TPU v7x, 256 devices: a whole 4x4x8 slice. The times are simulated.
256 devices in a mesh: req: 4 (over z_lo, core), exp: 64 (over y, x, z_hi).
Axes of the slice: x: 4, y: 4, z: 8 (z_hi: 4, z_lo: 2; z = z_hi * 2 + z_lo), core: 2. Of those that a mesh axis runs over, the one named last changes fastest.
Arguments:
- residual: bfloat16 [8192, 2048], P('exp'), may hold values from -6 to 6
- queries: bfloat16 [8192, 2048], P('exp', 'req'), may hold values from -128 to 128, as said below
- prefix_kv: bfloat16 [4, 16384, 256], P('req', 'exp'), may hold values from -4.5 to 4.5
- suffix_kv: bfloat16 [8192, 4, 256], P('exp', 'req'), may hold values from -6 to 6
- suffix_lengths: int32 [64, 4], P('exp'), may hold values from 1 to 96, 128 in all within a row
- out_proj: bfloat16 [2048, 2048], P('req'), may hold values from -0.5 to 0.5
- norm_gain: bfloat16 [2048], replicated, may hold values from 0.099609375 to 1.8984375
- routes: int32 [8192, 6], P('exp'), may hold values from 0 to 63, all different within a row; in each aligned block of 128 rows (0 to 127, 128 to 255, ...) at most 24 rows name the same one
- route_weights: float32 [8192, 6], P('exp'), may hold values from 0.1 to 0.5
- expert_gate: bfloat16 [64, 2048, 1408], P('exp', None, 'req'), may hold values from -0.125 to 0.125
- expert_up: bfloat16 [64, 2048, 1408], P('exp', None, 'req'), may hold values from -0.125 to 0.125
- expert_down: bfloat16 [64, 1408, 2048], P('exp', 'req'), may hold values from -0.15625 to 0.15625
- shared_gate: bfloat16 [2048, 1408], P(None, 'req'), may hold values from -0.125 to 0.125
- shared_up: bfloat16 [2048, 1408], P(None, 'req'), may hold values from -0.125 to 0.125
- shared_down: bfloat16 [1408, 2048], P('req'), may hold values from -0.15625 to 0.15625
Outputs:
- layer_out: bfloat16 [8192, 2048], P('exp')
Inputs may be any that keep to these rules, and one draw needn't show every extreme that they name: In the hidden draw some queries are strong multiples of prefix keys. `suffix_lengths`: each row (the requests of one index of exp) sums to 128, and in every row one request has exactly 96 tokens. `routes`: the 6 experts of a token are different. Among the 128 tokens of one index of exp no expert is picked more than 24 times, and in every draw some expert is picked exactly 24 times by the tokens of some index of exp.
All inputs are finite; a program needn't handle non-finite values.
Results may differ from a plain program's by a relative error of at most 0.015.
Values may be sent and summed in bfloat16 or wider, within the bound.
A program may use at most 128 MiB of HBM per device.

v0:
```python
import math
import jax
import jax.numpy as jnp
from jax import lax
from jax.sharding import PartitionSpec as P

HD = 128
TOP = 6
neg_big = -1e30
norm_eps = 1e-06


def on_device(
    residual,
    queries,
    prefix_kv,
    suffix_kv,
    suffix_lengths,
    out_proj,
    norm_gain,
    routes,
    route_weights,
    expert_gate,
    expert_up,
    expert_down,
    shared_gate,
    shared_up,
    shared_down,
):
    tokens_here = residual.shape[0]
    feat_width = residual.shape[1]
    head_count = queries.shape[1] // HD
    scaling = 1.0 / math.sqrt(HD)
    query_heads = jnp.transpose(queries.reshape(tokens_here, head_count, HD), (1, 0, 2))
    start_state = (
        jnp.full((head_count, tokens_here), neg_big, jnp.float32),
        jnp.zeros((head_count, tokens_here), jnp.float32),
        jnp.zeros((head_count, tokens_here, HD), jnp.float32),
    )

    def absorb(carried, key_rows, value_rows, allowed):
        running_max, running_sum, running_acc = carried
        scores = (
            jnp.einsum("htd,kd->htk", query_heads, key_rows, preferred_element_type=jnp.float32)
            * scaling
        )
        if allowed is not None:
            scores = jnp.where(allowed[None], scores, neg_big)
        new_max = jnp.maximum(running_max, jnp.max(scores, axis=-1))
        factor = jnp.exp(running_max - new_max)
        exp_scores = jnp.exp(scores - new_max[..., None])
        new_sum = running_sum * factor + jnp.sum(exp_scores, axis=-1)
        new_acc = running_acc * factor[..., None] + jnp.einsum(
            "htk,kd->htd",
            exp_scores.astype(jnp.bfloat16),
            value_rows,
            preferred_element_type=jnp.float32,
        )
        return (new_max, new_sum, new_acc)

    portion = lax.all_gather(prefix_kv, "exp", axis=1, tiled=True)
    key_count = portion.shape[1]
    window_len = math.gcd(key_count, 2048)

    def inner(position, inner_state):
        window = lax.dynamic_slice_in_dim(portion[0], position * window_len, window_len, 0)
        return absorb(inner_state, window[:, :HD], window[:, HD:], None)

    carried = lax.fori_loop(0, key_count // window_len, inner, start_state)
    request_ends = jnp.cumsum(suffix_lengths[0])
    positions = jnp.arange(tokens_here, dtype=jnp.int32)
    request_ids = jnp.sum((positions[:, None] >= request_ends[None, :]).astype(jnp.int32), axis=1)
    allowed = (request_ids[:, None] == request_ids[None, :]) & (
        positions[None, :] <= positions[:, None]
    )
    carried = absorb(carried, suffix_kv[:, 0, :HD], suffix_kv[:, 0, HD:], allowed)
    running_max, running_sum, running_acc = carried
    attention = (
        jnp.transpose(running_acc / running_sum[..., None], (1, 0, 2))
        .reshape(tokens_here, head_count * HD)
        .astype(jnp.bfloat16)
    )
    attn_terms = jnp.dot(attention, out_proj, preferred_element_type=jnp.float32)
    attn_out = lax.psum(attn_terms.astype(jnp.bfloat16), "req").astype(jnp.float32)
    hidden_state = (residual.astype(jnp.float32) + attn_out).astype(jnp.bfloat16)
    hidden_float = hidden_state.astype(jnp.float32)
    mean_square = jnp.mean(hidden_float * hidden_float, axis=-1, keepdims=True)
    normed = (
        hidden_float * lax.rsqrt(mean_square + norm_eps) * norm_gain.astype(jnp.float32)
    ).astype(jnp.bfloat16)
    shared_gate_act = jnp.dot(normed, shared_gate, preferred_element_type=jnp.float32)
    shared_up_act = jnp.dot(normed, shared_up, preferred_element_type=jnp.float32)
    shared_hidden = (jax.nn.silu(shared_gate_act) * shared_up_act).astype(jnp.bfloat16)
    shared_part = jnp.dot(shared_hidden, shared_down, preferred_element_type=jnp.float32)
    exp_count = lax.axis_size("exp")
    experts = exp_count * expert_gate.shape[0]
    capacity = min(tokens_here, 4 * ((tokens_here * TOP + 2 * experts - 1) // (2 * experts)))
    pick_ids = routes.reshape(-1)
    one_hot = (pick_ids[:, None] == jnp.arange(experts, dtype=jnp.int32)[None, :]).astype(jnp.int32)
    pick_ranks = jnp.sum((jnp.cumsum(one_hot, axis=0) - one_hot) * one_hot, axis=1)
    pick_slots = (pick_ids * capacity + pick_ranks).reshape(tokens_here, TOP)
    slot_ids = jnp.arange(experts * capacity, dtype=jnp.int32)
    placement = jnp.any(pick_slots[None, :, :] == slot_ids[:, None, None], axis=2).astype(
        jnp.bfloat16
    )
    buffer = (
        jnp.dot(placement, normed, preferred_element_type=jnp.float32)
        .astype(jnp.bfloat16)
        .reshape(experts, capacity, feat_width)
    )
    source_rows = lax.all_to_all(buffer, "exp", split_axis=0, concat_axis=0, tiled=True)
    sources, slot_count, row_width = source_rows.shape
    flat_rows = source_rows.reshape(sources * slot_count, row_width)
    gate_act = jnp.dot(flat_rows, expert_gate[0], preferred_element_type=jnp.float32)
    up_act = jnp.dot(flat_rows, expert_up[0], preferred_element_type=jnp.float32)
    expert_hidden = (jax.nn.silu(gate_act) * up_act).astype(jnp.bfloat16)
    partial_out = jnp.dot(expert_hidden, expert_down[0], preferred_element_type=jnp.float32).astype(
        jnp.bfloat16
    )
    finish_partial_out = partial_out.reshape(sources, slot_count, row_width)
    returned = lax.all_to_all(finish_partial_out, "exp", split_axis=0, concat_axis=0, tiled=True)
    flat_back = returned.reshape(experts * capacity, feat_width)
    picked_rows = (
        flat_back[pick_slots.reshape(-1)].astype(jnp.float32).reshape(tokens_here, TOP, feat_width)
    )
    routed = jnp.sum(picked_rows * route_weights[:, :, None], axis=1)
    summed = lax.psum((shared_part + routed).astype(jnp.bfloat16), "req").astype(jnp.float32)
    return (hidden_float + summed).astype(jnp.bfloat16)


def solution(mesh):
    placed = (
        P("exp", None),
        P("exp", "req"),
        P("req", "exp", None),
        P("exp", "req", None),
        P("exp", None),
        P("req", None),
        P(),
        P("exp", None),
        P("exp", None),
        P("exp", None, "req"),
        P("exp", None, "req"),
        P("exp", "req", None),
        P(None, "req"),
        P(None, "req"),
        P("req", None),
    )
    return jax.shard_map(
        on_device, mesh=mesh, in_specs=placed, out_specs=P("exp", None), check_vma=False
    )
```

profile of v0, /device:TPU:1, one launch (start us, length us, event | category | flops | bytes accessed | tf_op | source)
XLA Modules:
  0.0 634.4 jit_solution(8159375901670634559)
XLA Ops:
  14.6 2.2 fusion.53
  16.8 104.8 %all-gather.2.cloned.1.call-done = bf16[1,16384,256]{2,1,0:T(8,128)(2,1)} async-done(((bf16[1,256,256]{2,1,0:T(8,128)(2,1)}), bf16[1,16384,256]{2,1,0:T(8,128)(2,1)}) %all-gather.2.cloned.1.call-update) | async-done | bytes 8388624 | tf_op jit(solution)/shard_map/all_gather | solution.py:61
  121.6 67.1 %while.18 = (s32[]{:T(128)}, f32[4,128]{1,0:T(4,128)S(1)}, f32[4,128]{1,0:T(4,128)S(1)}, f32[4,128,128]{2,1,0:T(8,128)S(1)}, bf16[1,16384,256]{2,1,0:T(8,128)(2,...) while((s32[]{:T(128)}, f32[4,128]{1,0:T(4,128)S(1)}, ...), condition=%wide.region_3.0_spmd.clone, body=%wide.region_0.0_spmd.clone.sunk | while | flops 545458688 | bytes 33194172 | solution.py:69
  122.9 2.7 bitcast_reduce_fusion.2
  125.6 3.0 fusion.75
  131.3 2.7 bitcast_reduce_fusion.2
  134.0 3.0 fusion.75
  139.7 2.7 bitcast_reduce_fusion.2
  142.4 3.0 fusion.75
  148.1 2.7 bitcast_reduce_fusion.2
  150.8 3.0 fusion.75
  156.5 2.7 bitcast_reduce_fusion.2
  159.2 3.0 fusion.75
  164.9 2.7 bitcast_reduce_fusion.2
  167.6 3.0 fusion.75
  173.2 2.7 bitcast_reduce_fusion.2
  175.9 3.0 fusion.75
  181.6 2.7 bitcast_reduce_fusion.2
  184.3 3.0 fusion.75
  194.4 48.7 %all-reduce.3.cloned.1.call-done = bf16[128,2048]{1,0:T(8,128)(2,1)} async-done(((bf16[128,2048]{1,0:T(8,128)(2,1)}), bf16[128,2048]{1,0:T(8,128)(2,1)}) %all-reduce.3.cloned.1.call-update) | async-done | bytes 524304 | tf_op jit(solution)/shard_map/psum | solution.py:84
  247.5 126.4 %all_to_all.10 = bf16[64,24,2048]{2,1,0:T(8,128)(2,1)S(1)} all-to-all(bf16[64,24,2048]{2,1,0:T(8,128)(2,1)S(1)} %bitcast.103), channel_id=1, replica_groups=mesh['req'=4,'exp'=64] {'exp'}, dimensions={0} | all-to-all | bytes 12582912 | tf_op jit(solution)/shard_map/all_to_all | solution.py:111
  373.9 2.7 copy-done.3
  376.6 3.8 fusion.18
  380.4 12.3 %convolution_convert_fusion = bf16[1536,2048]{1,0:T(8,128)(2,1)} fusion(bf16[1,352,2048]{2,1,0:T(8,128)(2,1)} %param.28, bf16[1536,2048]{1,0:T(8,128)(2,1)} %bitcast.106, f32[1536,352]{0,1:T(8,128)} %fusion.18, bf16[1,2048,352]{1,2,0:T(8,128)(2,1)} %param.27), kind=kOutput, calls=%fused_computation.21 | convolution fusion | flops 4435574784 | bytes 17629184 | tf_op jit(solution)/shard_map/dot_general | solution.py:117
  392.7 8.7 %all-to-all-start.1 = ((bf16[64,24,2048]{2,1,0:T(8,128)(2,1)}), bf16[64,24,2048]{2,1,0:T(8,128)(2,1)}, u32[]{:S(2)}, u32[]{:S(2)}) async-start(bf16[64,24,2048]{2,1,0:T(8,128)(2,1)} %bitcast.104), calls=%async_computation.1 | async-start | bytes 12582912 | tf_op jit(solution)/shard_map/all_to_all | solution.py:121
  402.5 139.7 %all-to-all-done.1 = bf16[64,24,2048]{2,1,0:T(8,128)(2,1)} async-done(((bf16[64,24,2048]{2,1,0:T(8,128)(2,1)}), bf16[64,24,2048]{2,1,0:T(8,128)(2,1)}, u32[]{:S(2)}, u32[]{:S(2)}) %all-to-all-start.1) | async-done | bytes 6291488 | tf_op jit(solution)/shard_map/all_to_all | solution.py:121
  542.2 10.7 %gather_fusion = bf16[768,2048]{1,0:T(8,128)(2,1)} fusion(bf16[1536,2048]{1,0:T(8,128)(2,1)} %bitcast.18, s32[1024]{0:T(1024)S(1)} %pad_clamp_fusion), kind=kCustom, calls=%fused_computation | custom fusion | bytes 6294528 | tf_op jit(solution)/shard_map/gather | solution.py:124
  552.9 6.6 %reshape.163 = f32[128,6,2048]{2,1,0:T(8,128)} reshape(bf16[768,2048]{1,0:T(8,128)(2,1)} %gather_fusion) | data formatting | bytes 9437184 | tf_op jit(solution)/shard_map/convert_element_type | solution.py:124
  559.5 7.6 %multiply_reduce_fusion = f32[128,2048]{1,0:T(8,128)} fusion(f32[128,6,2048]{2,1,0:T(8,128)} %reshape.163, f32[128,6]{1,0:T(8,128)S(1)} %copy.46), kind=kLoop, calls=%fused_computation.20 | loop fusion | flops 2883584 | bytes 7343104 | tf_op jit(solution)/shard_map/reduce_sum | solution.py:126
  567.1 4.5 fusion.15
  571.6 54.0 %all-reduce.5.cloned.1.call-done = bf16[128,2048]{1,0:T(8,128)(2,1)} async-done(((bf16[128,2048]{1,0:T(8,128)(2,1)}), bf16[128,2048]{1,0:T(8,128)(2,1)}) %all-reduce.5.cloned.1.call-update) | async-done | bytes 524304 | tf_op jit(solution)/shard_map/psum | solution.py:127
  625.7 2.2 fusion.27
  (123 shorter events, 39.9 us)
Async XLA Ops:
  6.5 185.3 %copy-start = (bf16[512,2048]{1,0:T(8,128)(2,1)S(1)}, bf16[512,2048]{1,0:T(8,128)(2,1)}, u32[]{:S(2)}) copy-start(bf16[512,2048]{1,0:T(8,128)(2,1)} %param.22) | copy-start | bytes 6291460
  6.5 115.1 %all-gather.2.cloned.1.call-start = ((), (), s32[]{:S(2)}) async-start(), calls=%async_computation.2 | async-start | bytes 8519680 | tf_op jit(solution)/shard_map/all_gather | solution.py:61
  7.3 235.9 %all-reduce.3.cloned.1.call-start = ((), (), s32[]{:S(2)}) async-start(), calls=%async_computation.3 | async-start | bytes 1048576 | tf_op jit(solution)/shard_map/psum | solution.py:84
  8.1 3.6 copy-start.8
  13.5 108.1 %copy-start.5 = (s32[64,6,128]{2,0,1:T(8,128)}, s32[64,6,128]{2,0,1:T(8,128)S(1)}, u32[]{:S(2)}) copy-start(s32[64,6,128]{2,0,1:T(8,128)S(1)} %reduce-window.19) | copy-start | bytes 589828
  125.6 3.4 copy-start.2
  134.0 3.4 copy-start.2
  142.4 3.4 copy-start.2
  150.8 3.4 copy-start.2
  159.2 3.4 copy-start.2
  167.5 3.4 copy-start.2
  175.9 3.4 copy-start.2
  184.3 3.4 copy-start.2
  190.6 2.6 copy-start.6
  190.6 2.6 copy-start.11
  190.6 2.9 copy-start.9
  191.8 51.3 %copy-start.4 = (bf16[128,2048]{1,0:T(8,128)(2,1)S(1)}, bf16[128,2048]{1,0:T(8,128)(2,1)}, u32[]{:S(2)}) copy-start(bf16[128,2048]{1,0:T(8,128)(2,1)} %param.17) | copy-start | bytes 1572868
  191.8 52.6 %copy-start.10 = (f32[2048]{0:T(1024)S(1)}, f32[2048]{0:T(1024)}, u32[]{:S(2)}) copy-start(f32[2048]{0:T(1024)} %convert_element_type.89) | copy-start | bytes 24580
  247.5 129.1 %copy-start.13 = (bf16[1,2048,352]{1,2,0:T(8,128)(2,1)S(1)}, bf16[1,2048,352]{1,2,0:T(8,128)(2,1)}, u32[]{:S(2)}) copy-start(bf16[1,2048,352]{1,2,0:T(8,128)(2,1)} %param.26) | copy-start | bytes 4325380
  373.9 2.7 copy-start.3
  392.7 9.1 %copy-start.12 = (f32[128,6]{0,1:T(8,128)S(1)}, f32[128,6]{0,1:T(8,128)}, u32[]{:S(2)}) copy-start(f32[128,6]{0,1:T(8,128)} %param.25) | copy-start | bytes 9220
  392.7 9.3 %copy-start.7 = (bf16[2048,352]{0,1:T(8,128)(2,1)S(1)}, bf16[2048,352]{0,1:T(8,128)(2,1)}, u32[]{:S(2)}) copy-start(bf16[2048,352]{0,1:T(8,128)(2,1)} %param.29) | copy-start | bytes 4325380
  392.7 149.6 %all-to-all-start.1 = ((bf16[64,24,2048]{2,1,0:T(8,128)(2,1)}), bf16[64,24,2048]{2,1,0:T(8,128)(2,1)}, u32[]{:S(2)}, u32[]{:S(2)}) async-start(bf16[64,24,2048]{2,1,0:T(8,128)(2,1)} %bitcast.104), calls=%async_computation.1 | async-start | bytes 12582912 | tf_op jit(solution)/shard_map/all_to_all | solution.py:121
  401.4 224.3 %all-reduce.5.cloned.1.call-start = ((), (), s32[]{:S(2)}) async-start(), calls=%async_computation.4 | async-start | bytes 1048576 | tf_op jit(solution)/shard_map/psum | solution.py:127
  567.1 60.8 %copy-start.1 = (bf16[512,2048]{1,0:T(8,128)(2,1)S(1)}, bf16[512,2048]{1,0:T(8,128)(2,1)}, u32[]{:S(2)}) copy-start(bf16[512,2048]{1,0:T(8,128)(2,1)} %param.22) | copy-start | bytes 6291460
Sparse Core Ops, SparseCore 0:
  10.6 110.9 all-gather.1
  193.3 49.7 all-reduce.2
  571.8 53.8 all-reduce.4
where the time goes:
time: 635 us; the launch traced here: 634 us
  waiting for transfers between devices  348 us (55%)
  blocking collectives  126 us (20%)
  matrix products  56.4 us (9%)
  other arithmetic  44.3 us (7%)
  local copies, waits for them, and re-layouts  36.5 us (6%)
  between operations  13.4 us (2%)
  starting transfers between devices  8.99 us (1%)
    all_to_all x1, waiting for transfers between devices, on_device(): lax.all_to_all(finish_partial_out, 'exp', split_axis=0, concat_axis=0, ti...  140 us
    all_to_all x1, blocking collectives, on_device(): lax.all_to_all(buffer, 'exp', split_axis=0, concat_axis=0, tiled=True)  126 us
    all_gather x1, waiting for transfers between devices, on_device(): portion = lax.all_gather(prefix_kv, 'exp', axis=1, tiled=True)  105 us
    psum x1, waiting for transfers between devices, on_device(): lax.psum((shared_part + routed).astype(jnp.bfloat16), 'req')  54 us
    psum x1, waiting for transfers between devices, on_device(): lax.psum(attn_terms.astype(jnp.bfloat16), 'req').astype(jnp.float32)  48.7 us
    reduce_sum x9, other arithmetic, absorb(): new_sum = running_sum * factor + jnp.sum(exp_scores, axis=-1)  25.3 us
    dot_general x9, matrix products, absorb(): jnp.einsum('htd,kd->htk', query_heads, key_rows, preferred_element_type=j...  23.7 us
  transfers between devices with their start and end apart: 4, of which 4 were waited for; matrix products, arithmetic and copies ran while one was open for 2% of the time, Pallas kernels for 0%

commit v1 on v0

--- a/solution.py
+++ b/solution.py
@@ -58,7 +58,9 @@
         )
         return (new_max, new_sum, new_acc)
 
-    portion = lax.all_gather(prefix_kv, "exp", axis=1, tiled=True)
+    portion = jnp.concatenate(
+        lax.all_to_all(jnp.stack([prefix_kv] * lax.axis_size("exp")), "exp", 0, 0), axis=1
+    )
     key_count = portion.shape[1]
     window_len = math.gcd(key_count, 2048)
 

time: 635 us -> 733 us (1.15)
  waiting for transfers between devices: 348 us -> 419 us
  matrix products: 56.4 us -> 81.4 us
  starting transfers between devices: 8.99 us -> 24.5 us
  local copies, waits for them, and re-layouts: 36.5 us -> 27.4 us
    all_to_all x0 -> x1, waiting for transfers between devices: none -> 175 us  [on_device(): lax.all_to_all(jnp.stack([prefix_kv] * lax.axis_size('exp')), 'exp', 0, 0)]
    all_gather x1 -> x0, waiting for transfers between devices: 105 us -> none  [on_device(): portion = lax.all_gather(prefix_kv, 'exp', axis=1, tiled=True)]
    dot_general x9, matrix products: 8.56 us -> 26.7 us  [absorb(): jnp.einsum('htk,kd->htd', exp_scores.astype(jnp.bfloat16), value_rows, pr...]
    all_to_all x0 -> x1, starting transfers between devices: none -> 15.5 us  [on_device(): lax.all_to_all(jnp.stack([prefix_kv] * lax.axis_size('exp')), 'exp', 0, 0)]
    dynamic_slice x8 -> x0, local copies, waits for them, and re-layouts: 10.4 us -> none  [inner(): lax.dynamic_slice_in_dim(portion[0], position * window_len, window_len, 0)]
  transfers between devices with their start and end apart: 4 -> 4, of which waited for: 4 -> 4; matrix products, arithmetic and copies ran while one was open for 2% -> 1% of each run, Pallas kernels for 0% -> 0%
where the time goes in v1:
time: 733 us; the launch traced here: 732 us
  waiting for transfers between devices  419 us (57%)
  blocking collectives  126 us (17%)
  matrix products  81.4 us (11%)
  other arithmetic  40 us (5%)
  local copies, waits for them, and re-layouts  27.4 us (4%)
  starting transfers between devices  24.5 us (3%)
  between operations  13.7 us (2%)
    all_to_all x1, waiting for transfers between devices, on_device(): lax.all_to_all(jnp.stack([prefix_kv] * lax.axis_size('exp')), 'exp', 0, 0)  175 us
    all_to_all x1, waiting for transfers between devices, on_device(): lax.all_to_all(finish_partial_out, 'exp', split_axis=0, concat_axis=0, ti...  139 us
    all_to_all x1, blocking collectives, on_device(): lax.all_to_all(buffer, 'exp', split_axis=0, concat_axis=0, tiled=True)  126 us
    psum x1, waiting for transfers between devices, on_device(): lax.psum((shared_part + routed).astype(jnp.bfloat16), 'req')  56.8 us
    psum x1, waiting for transfers between devices, on_device(): lax.psum(attn_terms.astype(jnp.bfloat16), 'req').astype(jnp.float32)  47.9 us
    dot_general x9, matrix products, absorb(): jnp.einsum('htd,kd->htk', query_heads, key_rows, preferred_element_type=j...  30.7 us
    dot_general x9, matrix products, absorb(): jnp.einsum('htk,kd->htd', exp_scores.astype(jnp.bfloat16), value_rows, pr...  26.7 us
    reduce_sum x9, other arithmetic, absorb(): new_sum = running_sum * factor + jnp.sum(exp_scores, axis=-1)  24.1 us
  transfers between devices with their start and end apart: 4, of which 4 were waited for; matrix products, arithmetic and copies ran while one was open for 1% of the time, Pallas kernels for 0%

profile of v1, /device:TPU:1, one launch (start us, length us, event | category | flops | bytes accessed | tf_op | source)
XLA Modules:
  0.0 732.2 jit_solution(4102215810174382764)
XLA Ops:
  6.5 5.3 stack.2
  11.8 15.5 %all-to-all-start = ((bf16[64,1,256,256]{3,2,1,0:T(8,128)(2,1)}), bf16[64,1,256,256]{3,2,1,0:T(8,128)(2,1)}, u32[]{:S(2)}, u32[]{:S(2)}) async-start(bf16[64,1,256,256]{3,2,1,0:T(8,128)(2,1)} %stack.2), calls=%async_computation | async-start | bytes 16777216 | tf_op jit(solution)/shard_map/all_to_all | solution.py:62
  31.5 175.4 %all-to-all-done = bf16[64,1,256,256]{3,2,1,0:T(8,128)(2,1)} async-done(((bf16[64,1,256,256]{3,2,1,0:T(8,128)(2,1)}), bf16[64,1,256,256]{3,2,1,0:T(8,128)(2,1)}, u32[]{:S(2)}, u32[]{:S(2)}) %all-to-all-start) | async-done | bytes 8388640 | tf_op jit(solution)/shard_map/all_to_all | solution.py:62
  206.9 78.9 %while.18 = (s32[]{:T(128)}, f32[4,128]{1,0:T(4,128)S(1)}, f32[4,128]{1,0:T(4,128)S(1)}, f32[4,128,128]{2,1,0:T(8,128)S(1)}, bf16[64,1,256,256]{3,2,0,1:T(8,128)...) while((s32[]{:T(128)}, f32[4,128]{1,0:T(4,128)S(1)}, ...), condition=%wide.region_3.0_spmd.clone, body=%wide.region_0.0_spmd.clone.sunk | while | flops 545458688 | bytes 14319807 | solution.py:71
  206.9 3.7 bitcast_reduce_fusion.2
  210.6 2.9 fusion.76
  213.5 3.2 fusion.78
  216.7 3.7 bitcast_reduce_fusion.2
  223.3 3.2 fusion.78
  226.6 3.7 bitcast_reduce_fusion.2
  233.2 3.2 fusion.78
  236.4 3.7 bitcast_reduce_fusion.2
  243.1 3.2 fusion.78
  246.3 3.7 bitcast_reduce_fusion.2
  252.9 3.2 fusion.78
  256.2 3.7 bitcast_reduce_fusion.2
  262.8 3.2 fusion.78
  266.0 3.7 bitcast_reduce_fusion.2
  272.6 3.2 fusion.78
  275.9 3.7 bitcast_reduce_fusion.2
  282.5 3.2 fusion.78
  291.3 47.9 %all-reduce.3.cloned.1.call-done = bf16[128,2048]{1,0:T(8,128)(2,1)} async-done(((bf16[128,2048]{1,0:T(8,128)(2,1)}), bf16[128,2048]{1,0:T(8,128)(2,1)}) %all-reduce.3.cloned.1.call-update) | async-done | bytes 524304 | tf_op jit(solution)/shard_map/psum | solution.py:86
  343.6 126.2 %all_to_all.15 = bf16[64,24,2048]{2,1,0:T(8,128)(2,1)S(1)} all-to-all(bf16[64,24,2048]{2,1,0:T(8,128)(2,1)S(1)} %bitcast.104), channel_id=1, replica_groups=mesh['req'=4,'exp'=64] {'exp'}, dimensions={0} | all-to-all | bytes 12582912 | tf_op jit(solution)/shard_map/all_to_all | solution.py:113
  472.5 3.8 fusion.19
  476.4 12.3 %convolution_convert_fusion = bf16[1536,2048]{1,0:T(8,128)(2,1)} fusion(bf16[1,352,2048]{2,1,0:T(8,128)(2,1)} %param.28, bf16[1536,2048]{1,0:T(8,128)(2,1)} %bitcast.107, f32[1536,352]{0,1:T(8,128)} %fusion.19, bf16[1,2048,352]{1,2,0:T(8,128)(2,1)} %param.27), kind=kOutput, calls=%fused_computation.21 | convolution fusion | flops 4435574784 | bytes 17629184 | tf_op jit(solution)/shard_map/dot_general | solution.py:119
  488.6 8.6 %all-to-all-start.2 = ((bf16[64,24,2048]{2,1,0:T(8,128)(2,1)}), bf16[64,24,2048]{2,1,0:T(8,128)(2,1)}, u32[]{:S(2)}, u32[]{:S(2)}) async-start(bf16[64,24,2048]{2,1,0:T(8,128)(2,1)} %bitcast.105), calls=%async_computation.2 | async-start | bytes 12582912 | tf_op jit(solution)/shard_map/all_to_all | solution.py:123
  498.4 138.5 %all-to-all-done.2 = bf16[64,24,2048]{2,1,0:T(8,128)(2,1)} async-done(((bf16[64,24,2048]{2,1,0:T(8,128)(2,1)}), bf16[64,24,2048]{2,1,0:T(8,128)(2,1)}, u32[]{:S(2)}, u32[]{:S(2)}) %all-to-all-start.2) | async-done | bytes 6291488 | tf_op jit(solution)/shard_map/all_to_all | solution.py:123
  636.9 10.7 %gather_fusion = bf16[768,2048]{1,0:T(8,128)(2,1)} fusion(bf16[1536,2048]{1,0:T(8,128)(2,1)} %bitcast.20, s32[1024]{0:T(1024)S(1)} %pad_clamp_fusion), kind=kCustom, calls=%fused_computation | custom fusion | bytes 6294528 | tf_op jit(solution)/shard_map/gather | solution.py:126
  647.6 6.6 reshape.163
  654.2 7.8 %multiply_reduce_fusion = f32[128,2048]{1,0:T(8,128)} fusion(f32[128,6,2048]{2,1,0:T(8,128)} %reshape.163, f32[128,6]{1,0:T(8,128)S(1)} %copy.60), kind=kLoop, calls=%fused_computation.20 | loop fusion | flops 2883584 | bytes 7343104 | tf_op jit(solution)/shard_map/reduce_sum | solution.py:128
  661.9 4.4 fusion.16
  666.3 56.8 %all-reduce.5.cloned.1.call-done = bf16[128,2048]{1,0:T(8,128)(2,1)} async-done(((bf16[128,2048]{1,0:T(8,128)(2,1)}), bf16[128,2048]{1,0:T(8,128)(2,1)}) %all-reduce.5.cloned.1.call-update) | async-done | bytes 524304 | tf_op jit(solution)/shard_map/psum | solution.py:129
  (97 shorter events, 40.3 us)
Async XLA Ops:
  6.5 282.3 %copy-start = (bf16[512,2048]{1,0:T(8,128)(2,1)S(1)}, bf16[512,2048]{1,0:T(8,128)(2,1)}, u32[]{:S(2)}) copy-start(bf16[512,2048]{1,0:T(8,128)(2,1)} %param.22) | copy-start | bytes 6291460
  11.8 15.6 %copy-start.7 = (s32[128,6]{0,1:T(8,128)S(1)}, s32[128,6]{0,1:T(8,128)}, u32[]{:S(2)}) copy-start(s32[128,6]{0,1:T(8,128)} %param.24) | copy-start | bytes 9220
  11.8 16.0 %copy-start.5 = (bf16[128,512]{1,0:T(8,128)(2,1)S(1)}, bf16[128,512]{1,0:T(8,128)(2,1)}, u32[]{:S(2)}) copy-start(bf16[128,512]{1,0:T(8,128)(2,1)} %param.18) | copy-start | bytes 393220
  11.8 16.3 %copy-start.11 = (s32[1,4]{1,0:T(1,128)S(1)}, s32[1,4]{1,0:T(1,128)}, u32[]{:S(2)}) copy-start(s32[1,4]{1,0:T(1,128)} %param.21) | copy-start | bytes 52
  11.8 16.5 %copy-start.8 = (bf16[2048]{0:T(1024)(128)(2,1)S(1)}, bf16[2048]{0:T(1024)(128)(2,1)}, u32[]{:S(2)}) copy-start(bf16[2048]{0:T(1024)(128)(2,1)} %param.23) | copy-start | bytes 12292
  11.8 18.8 %copy-start.6 = (bf16[128,1,256]{2,0,1:T(8,128)(2,1)S(1)}, bf16[128,1,256]{2,0,1:T(8,128)(2,1)}, u32[]{:S(2)}) copy-start(bf16[128,1,256]{2,0,1:T(8,128)(2,1)} %param.20) | copy-start | bytes 196612
  11.8 195.0 %all-to-all-start = ((bf16[64,1,256,256]{3,2,1,0:T(8,128)(2,1)}), bf16[64,1,256,256]{3,2,1,0:T(8,128)(2,1)}, u32[]{:S(2)}, u32[]{:S(2)}) async-start(bf16[64,1,256,256]{3,2,1,0:T(8,128)(2,1)} %stack.2), calls=%async_computation | async-start | bytes 16777216 | tf_op jit(solution)/shard_map/all_to_all | solution.py:62
  27.4 311.9 %all-reduce.3.cloned.1.call-start = ((), (), s32[]{:S(2)}) async-start(), calls=%async_computation.3 | async-start | bytes 1048576 | tf_op jit(solution)/shard_map/psum | solution.py:86
  285.7 53.6 %copy-start.3 = (bf16[128,2048]{1,0:T(8,128)(2,1)S(1)}, bf16[128,2048]{1,0:T(8,128)(2,1)}, u32[]{:S(2)}) copy-start(bf16[128,2048]{1,0:T(8,128)(2,1)} %param.17) | copy-start | bytes 1572868
  343.6 128.9 %copy-start.10 = (bf16[1,2048,352]{1,2,0:T(8,128)(2,1)S(1)}, bf16[1,2048,352]{1,2,0:T(8,128)(2,1)}, u32[]{:S(2)}) copy-start(bf16[1,2048,352]{1,2,0:T(8,128)(2,1)} %param.26) | copy-start | bytes 4325380
  469.9 2.7 copy-start.2
  488.6 9.1 %copy-start.9 = (f32[128,6]{0,1:T(8,128)S(1)}, f32[128,6]{0,1:T(8,128)}, u32[]{:S(2)}) copy-start(f32[128,6]{0,1:T(8,128)} %param.25) | copy-start | bytes 9220
  488.6 9.2 %copy-start.4 = (bf16[2048,352]{0,1:T(8,128)(2,1)S(1)}, bf16[2048,352]{0,1:T(8,128)(2,1)}, u32[]{:S(2)}) copy-start(bf16[2048,352]{0,1:T(8,128)(2,1)} %param.29) | copy-start | bytes 4325380
  488.6 148.3 %all-to-all-start.2 = ((bf16[64,24,2048]{2,1,0:T(8,128)(2,1)}), bf16[64,24,2048]{2,1,0:T(8,128)(2,1)}, u32[]{:S(2)}, u32[]{:S(2)}) async-start(bf16[64,24,2048]{2,1,0:T(8,128)(2,1)} %bitcast.105), calls=%async_computation.2 | async-start | bytes 12582912 | tf_op jit(solution)/shard_map/all_to_all | solution.py:123
  497.3 225.8 %all-reduce.5.cloned.1.call-start = ((), (), s32[]{:S(2)}) async-start(), calls=%async_computation.4 | async-start | bytes 1048576 | tf_op jit(solution)/shard_map/psum | solution.py:129
  654.2 71.2 %copy-start.1 = (bf16[512,2048]{1,0:T(8,128)(2,1)S(1)}, bf16[512,2048]{1,0:T(8,128)(2,1)}, u32[]{:S(2)}) copy-start(bf16[512,2048]{1,0:T(8,128)(2,1)} %param.22) | copy-start | bytes 6291460
Sparse Core Ops, SparseCore 0:
  290.3 48.9 all-reduce.2
  666.4 56.6 all-reduce.4
